TPU v7x, 512 devices: a whole 4x8x8 slice. The times are simulated.
512 devices in a mesh: grp: 16 (over y, core), path: 32 (over z, x).
Axes of the slice: x: 4, y: 8, z: 8, core: 2. Of those that a mesh axis runs over, the one named last changes fastest.
Arguments:
- link_state: bfloat16 [16, 16384, 256], P('grp', 'path'), may hold values from -6 to 6
- path_state: bfloat16 [16, 4096, 256], P('grp', 'path'), may hold values from -6 to 6
- path_links: int32 [4096, 8], P('path'), may hold values from -1 to 16383, as said below
- w_path_in: bfloat16 [256, 768], replicated, may hold values from -0.375 to 0.375
- w_path_hid: bfloat16 [256, 768], replicated, may hold values from -0.375 to 0.375
- w_link_in: bfloat16 [256, 768], replicated, may hold values from -0.375 to 0.375
- w_link_hid: bfloat16 [256, 768], replicated, may hold values from -0.375 to 0.375
- cotangent: bfloat16 [16, 4096, 128], P('grp', 'path'), may hold values from -0.0234375 to 0.0234375
Outputs:
- link_next: bfloat16 [16, 16384, 256], P('grp', 'path')
- path_final: bfloat16 [16, 4096, 256], P('grp', 'path')
- read_grad: float32 [128, 256], P('path')
Inputs may be any that keep to these rules, and one draw needn't show every extreme that they name: `path_links`: entry -1 marks no hop; each path's live entries come first and number two or more. In the rows of one device, at most 32 live entries name links of the block of 512 link ids held by any one index of path, and some block takes exactly 32.
All inputs are finite; a program needn't handle non-finite values.
Results may differ from a plain program's by a relative error of at most 0.0035.
Values may be sent and summed in bfloat16 or wider, within the bound.
A program may use at most 64 MiB of HBM per device.

v0:
```python
import jax
import jax.numpy as jnp
from jax import lax
from jax.sharding import PartitionSpec as P


def gated_update(projected, carried, w_hidden):
    width = carried.shape[1]
    recur = jnp.dot(carried.astype(jnp.bfloat16), w_hidden, preferred_element_type=jnp.float32)
    reset = jax.nn.sigmoid(projected[:, :width] + recur[:, :width])
    update = jax.nn.sigmoid(projected[:, width : 2 * width] + recur[:, width : 2 * width])
    candidate = jnp.tanh(projected[:, 2 * width :] + reset * recur[:, 2 * width :])
    return (1.0 - update) * candidate + update * carried


def shards(
    link_state, path_state, path_links, w_path_in, w_path_hid, w_link_in, w_link_hid, cotangent
):
    own_links = link_state[0]
    link_dev, width = own_links.shape
    peer_count = lax.axis_size("path")
    path_count, hop_count = path_links.shape
    flat_ids = path_links.reshape(-1)
    is_live = flat_ids >= 0
    owner_id = jnp.where(is_live, flat_ids // link_dev, peer_count)
    local_id = jnp.where(is_live, flat_ids % link_dev, -1)
    capacity = flat_ids.shape[0] // peer_count
    marks = (owner_id[:, None] == jnp.arange(peer_count)[None, :]).astype(jnp.int32)
    slot_id = jnp.sum((jnp.cumsum(marks, axis=0) - marks) * marks, axis=1)
    requests = (
        jnp.full((peer_count, capacity), -1, jnp.int32)
        .at[owner_id, slot_id]
        .set(local_id, mode="drop")
    )
    nothing = jnp.zeros((), jnp.bfloat16)
    every_link = lax.all_gather(own_links, "path", axis=0, tiled=True)
    fetched = jnp.where(is_live[:, None], every_link[jnp.where(is_live, flat_ids, 0)], nothing)
    received = lax.all_to_all(requests, "path", split_axis=0, concat_axis=0, tiled=True)
    projected = jnp.dot(fetched, w_path_in, preferred_element_type=jnp.float32)
    projected = projected.reshape(path_count, hop_count, 3 * width)
    live_grid = is_live.reshape(path_count, hop_count)
    carried = path_state[0].astype(jnp.float32)
    messages = []
    for hop_index in range(hop_count):
        renewed = gated_update(projected[:, hop_index], carried, w_path_hid)
        carried = jnp.where(live_grid[:, hop_index, None], renewed, carried)
        messages.append(carried.astype(jnp.bfloat16))
    path_final = carried.astype(jnp.bfloat16)
    flat_messages = jnp.stack(messages, axis=1).reshape(-1, width)
    outgoing = (
        jnp.zeros((peer_count, capacity, width), jnp.bfloat16)
        .at[owner_id, slot_id]
        .set(flat_messages, mode="drop")
    )
    incoming = lax.all_to_all(outgoing, "path", split_axis=0, concat_axis=0, tiled=True)
    selector = (received.reshape(-1)[None, :] == jnp.arange(link_dev)[:, None]).astype(jnp.bfloat16)
    link_sum = jnp.dot(selector, incoming.reshape(-1, width), preferred_element_type=jnp.float32)
    link_proj = jnp.dot(
        link_sum.astype(jnp.bfloat16), w_link_in, preferred_element_type=jnp.float32
    )
    link_next = gated_update(link_proj, own_links.astype(jnp.float32), w_link_hid).astype(
        jnp.bfloat16
    )
    grad_term = lax.dot_general(
        cotangent[0], path_final, (((0,), (0,)), ((), ())), preferred_element_type=jnp.float32
    )
    grad_whole = lax.psum(grad_term, ("grp", "path"))
    share = grad_whole.shape[0] // peer_count
    read_grad = lax.dynamic_slice_in_dim(grad_whole, lax.axis_index("path") * share, share, 0)
    return (link_next[None], path_final[None], read_grad)


def solution(mesh):
    return jax.shard_map(
        shards,
        mesh=mesh,
        in_specs=(
            P("grp", "path", None),
            P("grp", "path", None),
            P("path", None),
            P(),
            P(),
            P(),
            P(),
            P("grp", "path", None),
        ),
        out_specs=(P("grp", "path", None), P("grp", "path", None), P("path", None)),
        check_vma=False,
    )
```

profile of v0, /device:TPU:1, one launch (start us, length us, event | category | flops | bytes accessed | tf_op | source)
XLA Modules:
  0.0 428.5 jit_solution(9627529892946809395)
XLA Ops:
  7.2 0.0 copy-start
  7.2 0.0 copy-start.1
  7.2 0.0 all-gather.3.cloned.1.call-start
  7.2 0.7 all-gather.3.cloned.1.call-update
  7.9 0.8 copy.20
  8.7 0.1 reshape.190
  8.8 0.1 reshape.189
  8.9 0.1 reshape.188
  9.0 9.0 %reduce-window.6 = s32[32,8,128]{2,1,0:T(8,128)S(1)} reduce-window(s32[32,8,128]{2,1,0:T(8,128)S(1)} %fusion.135, s32[]{:T(128)} %constant.44.clone.1), window={size=1x1x128 pad=0_0x0_0x127_0}, to_apply=%region_0.1 | reduce-window | flops 4161536 | bytes 262148 | tf_op jit(solution)/shard_map/reduce-window
  18.0 0.1 slice.290
  18.1 0.1 copy.23
  18.3 0.1 copy.24
  18.4 0.1 broadcast_add_fusion
  18.6 0.7 multiply_reduce_fusion
  19.4 4.3 %scatter_custom_fusion = s32[1024]{0:T(1024)S(1)} fusion(s32[1024]{0:T(1024)S(1)} %broadcast_select_fusion, s32[1024]{0:T(1024)S(1)} %get-tuple-element.33, s32[]{:T(128)} %constant.26.clone.1), kind=kCustom, calls=%fused_computation.239 | custom fusion | bytes 4100
  23.7 0.7 all_to_all.9
  24.4 13.7 %all-to-all-start = ((s32[32,1,32]{2,1,0:T(1,128)}), s32[32,1,32]{2,1,0:T(1,128)S(1)}, u32[]{:S(2)}, u32[]{:S(2)}) async-start(s32[32,1,32]{2,1,0:T(1,128)} %all_to_all.9), calls=%async_computation | async-start | bytes 32768 | tf_op jit(solution)/shard_map/all_to_all | solution.py:38
  38.1 0.7 broadcast_compare_fusion
  38.9 0.0 copy-done.1
  38.9 1.1 fusion.136
  39.9 80.9 %all-gather.3.cloned.1.call-done = bf16[1,16384,256]{2,1,0:T(8,128)(2,1)} async-done(((bf16[1,512,256]{2,1,0:T(8,128)(2,1)}), bf16[1,16384,256]{2,1,0:T(8,128)(2,1)}) %all-gather.3.cloned.1.call-update) | async-done | bytes 8388624 | tf_op jit(solution)/shard_map/all_gather | solution.py:36
  120.9 7.9 %gather_fusion = bf16[1024,256]{1,0:T(8,128)(2,1)S(1)} fusion(bf16[16384,256]{1,0:T(8,128)(2,1)} %bitcast.116, s32[1024]{0:T(1024)S(1)} %broadcast_clamp_fusion), kind=kCustom, calls=%fused_computation | custom fusion | bytes 1052672 | tf_op jit(solution)/shard_map/gather | solution.py:37
  128.8 0.0 copy-done
  128.8 0.6 convolution_bitcast_fusion
  129.4 0.0 copy-start.5
  129.5 2.1 fusion.170
  131.6 0.0 copy-done.5
  131.7 0.1 bitcast_dynamic-update-slice_fusion.7
  131.8 0.2 fusion.151
  132.0 0.1 bitcast_dynamic-update-slice_fusion.6
  132.2 0.2 fusion.149
  132.4 0.1 bitcast_dynamic-update-slice_fusion.5
  132.5 0.2 fusion.147
  132.8 0.1 bitcast_dynamic-update-slice_fusion.4
  132.9 0.2 fusion.145
  133.2 0.1 bitcast_dynamic-update-slice_fusion.3
  133.3 0.2 fusion.143
  133.5 0.1 bitcast_dynamic-update-slice_fusion.2
  133.6 0.2 fusion.141
  133.9 0.1 bitcast_dynamic-update-slice_fusion.1
  134.0 0.2 fusion.139
  134.2 0.0 copy-start.6
  134.3 0.0 copy-start.2
  134.3 0.0 copy-start.3
  134.3 0.1 bitcast_dynamic-update-slice_fusion
  134.4 0.0 copy-start.4
  134.4 6.4 %scatter_custom_fusion.1 = bf16[1024,256]{1,0:T(8,128)(2,1)} fusion(s32[1024]{0:T(1024)S(1)} %broadcast_select_fusion, bf16[128,8,256]{2,0,1:T(8,128)(2,1)S(1)} %get-tuple-element.9, bf16[]{:T(256)} %constant.50.clone.1), kind=kCustom, calls=%fused_computation.26 | custom fusion | bytes 1048578
  140.8 0.0 all-to-all-done
  140.8 5.3 %all-to-all-start.1 = ((bf16[32,32,256]{2,1,0:T(8,128)(2,1)}), bf16[32,32,256]{2,1,0:T(8,128)(2,1)}, u32[]{:S(2)}, u32[]{:S(2)}) async-start(bf16[32,32,256]{2,1,0:T(8,128)(2,1)} %bitcast.32), calls=%async_computation.1 | async-start | bytes 1048576 | tf_op jit(solution)/shard_map/all_to_all | solution.py:55
  146.2 0.0 all-reduce.2.cloned.1.call-start
  146.2 0.0 copy-done.6
  146.2 0.9 convolution_bitcast_fusion.1
  147.1 0.0 copy-done.4
  147.1 0.0 all-reduce.2.cloned.1.call-update
  147.1 0.4 fusion.23
  147.5 0.5 broadcast.260
  148.0 0.7 reduce.9
  148.7 0.1 eq.44
  148.8 267.0 %all-reduce.2.cloned.1.call-done = f32[128,256]{0,1:T(8,128)} async-done(((f32[128,256]{0,1:T(8,128)}), f32[128,256]{0,1:T(8,128)}) %all-reduce.2.cloned.1.call-update) | async-done | bytes 131088 | tf_op jit(solution)/shard_map/psum | solution.py:67
  415.8 1.0 constant_dynamic-slice_fusion
  416.8 0.7 copy.34
  417.4 0.0 all-to-all-done.1
  417.4 2.2 fusion.2
  419.6 2.0 fusion.27
  (22 shorter events, 0.4 us)
Async XLA Ops:
  7.2 121.6 %copy-start = (bf16[256,768]{1,0:T(8,128)(2,1)S(1)}, bf16[256,768]{1,0:T(8,128)(2,1)}, u32[]{:S(2)}) copy-start(bf16[256,768]{1,0:T(8,128)(2,1)} %param.11) | copy-start | bytes 1179652
  7.2 31.7 %copy-start.1 = (bf16[256,768]{1,0:T(8,128)(2,1)S(1)}, bf16[256,768]{1,0:T(8,128)(2,1)}, u32[]{:S(2)}) copy-start(bf16[256,768]{1,0:T(8,128)(2,1)} %param.12) | copy-start | bytes 1179652
  7.2 113.7 %all-gather.3.cloned.1.call-start = ((), (), s32[]{:S(2)}) async-start(), calls=%async_computation.3 | async-start | bytes 8650752 | tf_op jit(solution)/shard_map/all_gather | solution.py:36
  24.4 116.4 %all-to-all-start = ((s32[32,1,32]{2,1,0:T(1,128)}), s32[32,1,32]{2,1,0:T(1,128)S(1)}, u32[]{:S(2)}, u32[]{:S(2)}) async-start(s32[32,1,32]{2,1,0:T(1,128)} %all_to_all.9), calls=%async_computation | async-start | bytes 32768 | tf_op jit(solution)/shard_map/all_to_all | solution.py:38
  129.4 2.2 copy-start.5
  134.2 12.0 %copy-start.6 = (bf16[1,128,128]{2,1,0:T(8,128)(2,1)S(1)}, bf16[1,128,128]{2,1,0:T(8,128)(2,1)}, u32[]{:S(2)}) copy-start(bf16[1,128,128]{2,1,0:T(8,128)(2,1)} %param.15) | copy-start | bytes 98308
  134.3 12.8 %copy-start.2 = (bf16[1,512,256]{2,1,0:T(8,128)(2,1)S(1)}, bf16[1,512,256]{2,1,0:T(8,128)(2,1)}, u32[]{:S(2)}) copy-start(bf16[1,512,256]{2,1,0:T(8,128)(2,1)} %param.8) | copy-start | bytes 786436
  134.3 12.8 %copy-start.3 = (bf16[256,768]{1,0:T(8,128)(2,1)S(1)}, bf16[256,768]{1,0:T(8,128)(2,1)}, u32[]{:S(2)}) copy-start(bf16[256,768]{1,0:T(8,128)(2,1)} %param.14) | copy-start | bytes 1179652
  134.4 12.6 %copy-start.4 = (bf16[128,256]{1,0:T(8,128)(2,1)}, bf16[128,256]{1,0:T(8,128)(2,1)S(1)}, u32[]{:S(2)}) copy-start(bf16[128,256]{1,0:T(8,128)(2,1)S(1)} %get-tuple-element.10) | copy-start | bytes 196612
  140.8 276.6 %all-to-all-start.1 = ((bf16[32,32,256]{2,1,0:T(8,128)(2,1)}), bf16[32,32,256]{2,1,0:T(8,128)(2,1)}, u32[]{:S(2)}, u32[]{:S(2)}) async-start(bf16[32,32,256]{2,1,0:T(8,128)(2,1)} %bitcast.32), calls=%async_computation.1 | async-start | bytes 1048576 | tf_op jit(solution)/shard_map/all_to_all | solution.py:55
  146.2 269.6 %all-reduce.2.cloned.1.call-start = ((), (), s32[]{:S(2)}) async-start(), calls=%async_computation.2 | async-start | bytes 262144 | tf_op jit(solution)/shard_map/psum | solution.py:67
Sparse Core Ops, SparseCore 0:
  11.2 109.6 all-gather.2
  152.6 263.1 all-reduce.1
where the time goes:
time: 429 us; the launch traced here: 428 us
  waiting for transfers between devices  349 us (81%)
  local copies, waits for them, and re-layouts  25.4 us (6%)
  starting transfers between devices  19.1 us (4%)
  between operations  14.5 us (3%)
  other arithmetic  14.4 us (3%)
  matrix products  6.55 us (2%)
    psum x1, waiting for transfers between devices, shards(): grad_whole = lax.psum(grad_term, ('grp', 'path'))  267 us
    all_gather x1, waiting for transfers between devices, shards(): every_link = lax.all_gather(own_links, 'path', axis=0, tiled=True)  80.9 us
    all_to_all x1, starting transfers between devices, shards(): lax.all_to_all(requests, 'path', split_axis=0, concat_axis=0, tiled=True)  13.7 us
    unnamed x26, local copies, waits for them, and re-layouts  12.4 us
    another operation x3, other arithmetic  9.14 us
  transfers between devices with their start and end apart: 4, of which 2 were waited for; matrix products, arithmetic and copies ran while one was open for 10% of the time, Pallas kernels for 0%

commit v1 on v0

--- a/solution.py
+++ b/solution.py
@@ -33,7 +33,15 @@
         .set(local_id, mode="drop")
     )
     nothing = jnp.zeros((), jnp.bfloat16)
-    every_link = lax.all_gather(own_links, "path", axis=0, tiled=True)
+    every_link = jnp.concatenate(
+        lax.all_to_all(
+            jnp.stack(tuple((own_links for _ in range(lax.psum(1, "path"))))),
+            "path",
+            split_axis=0,
+            concat_axis=0,
+        ),
+        axis=0,
+    )
     fetched = jnp.where(is_live[:, None], every_link[jnp.where(is_live, flat_ids, 0)], nothing)
     received = lax.all_to_all(requests, "path", split_axis=0, concat_axis=0, tiled=True)
     projected = jnp.dot(fetched, w_path_in, preferred_element_type=jnp.float32)

time: 429 us -> 542 us (1.26)
  waiting for transfers between devices: 349 us -> 440 us
  starting transfers between devices: 19.1 us -> 39.1 us
    all_to_all x0 -> x1, waiting for transfers between devices: none -> 172 us  [shards(): lax.all_to_all(jnp.stack(tuple((own_links for _ in range(lax.psum(1, 'pat...]
    all_gather x1 -> x0, waiting for transfers between devices: 80.9 us -> none  [shards(): every_link = lax.all_gather(own_links, 'path', axis=0, tiled=True)]
    all_to_all x0 -> x1, starting transfers between devices: none -> 14 us  [shards(): lax.all_to_all(jnp.stack(tuple((own_links for _ in range(lax.psum(1, 'pat...]
    unnamed x26 -> x30, local copies, waits for them, and re-layouts: 12.4 us -> 11.8 us
  transfers between devices with their start and end apart: 4 -> 4, of which waited for: 2 -> 2; matrix products, arithmetic and copies ran while one was open for 10% -> 7% of each run, Pallas kernels for 0% -> 0%
where the time goes in v1:
time: 542 us
  waiting for transfers between devices  440 us (81%)
  starting transfers between devices  39.1 us (7%)
  local copies, waits for them, and re-layouts  29.8 us (5%)
  between operations  14.5 us (3%)
  other arithmetic  13 us (2%)
  matrix products  5.71 us (1%)
    psum x1, waiting for transfers between devices, shards(): grad_whole = lax.psum(grad_term, ('grp', 'path'))  268 us
    all_to_all x1, waiting for transfers between devices, shards(): lax.all_to_all(jnp.stack(tuple((own_links for _ in range(lax.psum(1, 'pat...  172 us
    all_to_all x1, starting transfers between devices, shards(): lax.all_to_all(requests, 'path', split_axis=0, concat_axis=0, tiled=True)  15.7 us
    all_to_all x1, starting transfers between devices, shards(): lax.all_to_all(jnp.stack(tuple((own_links for _ in range(lax.psum(1, 'pat...  14 us
    unnamed x30, local copies, waits for them, and re-layouts  11.8 us
  transfers between devices with their start and end apart: 4, of which 2 were waited for; matrix products, arithmetic and copies ran while one was open for 7% of the time, Pallas kernels for 0%

profile of v1, /device:TPU:1, one launch (start us, length us, event | category | flops | bytes accessed | tf_op | source)
XLA Modules:
  0.0 542.0 jit_solution(5224355992175156507)
XLA Ops:
  7.2 0.0 copy-start
  7.2 5.2 stack.30
  12.3 14.0 %all-to-all-start.1 = ((bf16[32,512,256]{2,1,0:T(8,128)(2,1)}), bf16[32,512,256]{2,1,0:T(8,128)(2,1)}, u32[]{:S(2)}, u32[]{:S(2)}) async-start(bf16[32,512,256]{2,1,0:T(8,128)(2,1)} %stack.30), calls=%async_computation.1 | async-start | bytes 16777216 | tf_op jit(solution)/shard_map/all_to_all | solution.py:37
  26.3 0.0 copy-done.7
  26.4 0.1 copy.20
  26.5 0.1 reshape.194
  26.5 0.1 reshape.193
  26.6 0.1 reshape.192
  26.8 9.0 %reduce-window.6 = s32[32,8,128]{2,1,0:T(8,128)S(1)} reduce-window(s32[32,8,128]{2,1,0:T(8,128)S(1)} %fusion.133, s32[]{:T(128)} %constant.44.clone.1), window={size=1x1x128 pad=0_0x0_0x127_0}, to_apply=%region_0.1 | reduce-window | flops 4161536 | bytes 262148 | tf_op jit(solution)/shard_map/reduce-window
  35.8 0.1 slice.290
  35.9 0.1 copy.23
  36.1 0.1 copy.24
  36.2 0.1 broadcast_add_fusion
  36.4 0.0 copy-done.8
  36.4 0.1 multiply_reduce_fusion
  36.5 4.3 scatter_custom_fusion
  40.8 0.7 all_to_all.12
  41.5 0.0 copy-done.1
  41.6 0.0 copy-done.5
  41.6 0.2 fusion.134
  41.8 172.1 %all-to-all-done.1 = bf16[32,512,256]{2,1,0:T(8,128)(2,1)} async-done(((bf16[32,512,256]{2,1,0:T(8,128)(2,1)}), bf16[32,512,256]{2,1,0:T(8,128)(2,1)}, u32[]{:S(2)}, u32[]{:S(2)}) %all-to-all-start.1) | async-done | bytes 8388640 | tf_op jit(solution)/shard_map/all_to_all | solution.py:37
  213.9 15.7 %all-to-all-start = ((s32[32,1,32]{2,1,0:T(1,128)}), s32[32,1,32]{2,1,0:T(1,128)S(1)}, u32[]{:S(2)}, u32[]{:S(2)}) async-start(s32[32,1,32]{2,1,0:T(1,128)} %all_to_all.12), calls=%async_computation | async-start | bytes 32768 | tf_op jit(solution)/shard_map/all_to_all | solution.py:46
  229.6 7.9 %gather_fusion = bf16[1024,256]{1,0:T(8,128)(2,1)S(1)} fusion(bf16[16384,256]{1,0:T(8,128)(2,1)} %bitcast.5, s32[1024]{0:T(1024)S(1)} %broadcast_clamp_fusion), kind=kCustom, calls=%fused_computation | custom fusion | bytes 1052672 | tf_op jit(solution)/shard_map/gather | solution.py:45
  237.5 0.0 copy-done
  237.5 0.6 convolution_bitcast_fusion
  238.2 2.1 fusion.170
  240.3 0.1 bitcast_dynamic-update-slice_fusion.7
  240.5 0.2 fusion.149
  240.7 0.1 bitcast_dynamic-update-slice_fusion.6
  240.8 0.2 fusion.147
  241.1 0.1 bitcast_dynamic-update-slice_fusion.5
  241.2 0.2 fusion.145
  241.5 0.1 bitcast_dynamic-update-slice_fusion.4
  241.6 0.2 fusion.143
  241.8 0.1 bitcast_dynamic-update-slice_fusion.3
  242.0 0.2 fusion.141
  242.2 0.1 bitcast_dynamic-update-slice_fusion.2
  242.3 0.2 fusion.139
  242.6 0.1 bitcast_dynamic-update-slice_fusion.1
  242.7 0.2 fusion.137
  242.9 0.0 copy-start.6
  242.9 0.0 copy-start.2
  243.0 0.0 copy-start.3
  243.0 0.1 bitcast_dynamic-update-slice_fusion
  243.1 0.0 copy-start.4
  243.1 6.4 %scatter_custom_fusion.1 = bf16[1024,256]{1,0:T(8,128)(2,1)} fusion(s32[1024]{0:T(1024)S(1)} %broadcast_select_fusion, bf16[128,8,256]{2,0,1:T(8,128)(2,1)S(1)} %get-tuple-element.9, bf16[]{:T(256)} %constant.50.clone.1), kind=kCustom, calls=%fused_computation.26 | custom fusion | bytes 1048578
  249.5 0.0 all-to-all-done
  249.5 9.3 %all-to-all-start.2 = ((bf16[32,32,256]{2,1,0:T(8,128)(2,1)}), bf16[32,32,256]{2,1,0:T(8,128)(2,1)}, u32[]{:S(2)}, u32[]{:S(2)}) async-start(bf16[32,32,256]{2,1,0:T(8,128)(2,1)} %bitcast.33), calls=%async_computation.2 | async-start | bytes 1048576 | tf_op jit(solution)/shard_map/all_to_all | solution.py:63
  258.9 0.0 all-reduce.2.cloned.1.call-start
  258.9 0.0 copy-done.6
  258.9 0.9 convolution_bitcast_fusion.1
  259.8 0.0 copy-done.4
  259.8 0.0 all-reduce.2.cloned.1.call-update
  259.8 0.0 copy-done.2
  259.8 0.4 fusion.160
  260.2 0.5 broadcast.261
  260.7 0.7 reduce.9
  261.4 0.1 eq.44
  261.5 267.8 %all-reduce.2.cloned.1.call-done = f32[128,256]{0,1:T(8,128)} async-done(((f32[128,256]{0,1:T(8,128)}), f32[128,256]{0,1:T(8,128)}) %all-reduce.2.cloned.1.call-update) | async-done | bytes 131088 | tf_op jit(solution)/shard_map/psum | solution.py:75
  529.3 1.0 constant_dynamic-slice_fusion
  530.3 0.7 copy.34
  531.0 0.0 all-to-all-done.2
  531.0 2.2 fusion.2
  533.1 2.0 fusion.25
  (26 shorter events, 0.4 us)
Async XLA Ops:
  7.2 230.3 %copy-start = (bf16[256,768]{1,0:T(8,128)(2,1)S(1)}, bf16[256,768]{1,0:T(8,128)(2,1)}, u32[]{:S(2)}) copy-start(bf16[256,768]{1,0:T(8,128)(2,1)} %param.11) | copy-start | bytes 1179652
  12.3 14.0 %copy-start.7 = (s32[128,8]{0,1:T(8,128)S(1)}, s32[128,8]{0,1:T(8,128)}, u32[]{:S(2)}) copy-start(s32[128,8]{0,1:T(8,128)} %param.10) | copy-start | bytes 12292
  12.3 24.0 %copy-start.8 = (s32[2]{0:T(128)S(1)}, s32[2]{0:T(128)}, u32[]{:S(2)}) copy-start(s32[2]{0:T(128)} %constant.58) | copy-start | bytes 28
  12.3 29.2 %copy-start.1 = (bf16[256,768]{1,0:T(8,128)(2,1)S(1)}, bf16[256,768]{1,0:T(8,128)(2,1)}, u32[]{:S(2)}) copy-start(bf16[256,768]{1,0:T(8,128)(2,1)} %param.12) | copy-start | bytes 1179652
  12.3 29.2 %copy-start.5 = (bf16[1,128,256]{2,1,0:T(8,128)(2,1)S(1)}, bf16[1,128,256]{2,1,0:T(8,128)(2,1)}, u32[]{:S(2)}) copy-start(bf16[1,128,256]{2,1,0:T(8,128)(2,1)} %param.9) | copy-start | bytes 196612
  12.3 201.5 %all-to-all-start.1 = ((bf16[32,512,256]{2,1,0:T(8,128)(2,1)}), bf16[32,512,256]{2,1,0:T(8,128)(2,1)}, u32[]{:S(2)}, u32[]{:S(2)}) async-start(bf16[32,512,256]{2,1,0:T(8,128)(2,1)} %stack.30), calls=%async_computation.1 | async-start | bytes 16777216 | tf_op jit(solution)/shard_map/all_to_all | solution.py:37
  213.9 35.7 %all-to-all-start = ((s32[32,1,32]{2,1,0:T(1,128)}), s32[32,1,32]{2,1,0:T(1,128)S(1)}, u32[]{:S(2)}, u32[]{:S(2)}) async-start(s32[32,1,32]{2,1,0:T(1,128)} %all_to_all.12), calls=%async_computation | async-start | bytes 32768 | tf_op jit(solution)/shard_map/all_to_all | solution.py:46
  242.9 16.0 %copy-start.6 = (bf16[1,128,128]{2,1,0:T(8,128)(2,1)S(1)}, bf16[1,128,128]{2,1,0:T(8,128)(2,1)}, u32[]{:S(2)}) copy-start(bf16[1,128,128]{2,1,0:T(8,128)(2,1)} %param.15) | copy-start | bytes 98308
  242.9 16.9 %copy-start.2 = (bf16[1,512,256]{2,1,0:T(8,128)(2,1)S(1)}, bf16[1,512,256]{2,1,0:T(8,128)(2,1)}, u32[]{:S(2)}) copy-start(bf16[1,512,256]{2,1,0:T(8,128)(2,1)} %param.8) | copy-start | bytes 786436
  243.0 16.9 %copy-start.3 = (bf16[256,768]{1,0:T(8,128)(2,1)S(1)}, bf16[256,768]{1,0:T(8,128)(2,1)}, u32[]{:S(2)}) copy-start(bf16[256,768]{1,0:T(8,128)(2,1)} %param.14) | copy-start | bytes 1179652
  243.1 16.7 %copy-start.4 = (bf16[128,256]{1,0:T(8,128)(2,1)}, bf16[128,256]{1,0:T(8,128)(2,1)S(1)}, u32[]{:S(2)}) copy-start(bf16[128,256]{1,0:T(8,128)(2,1)S(1)} %get-tuple-element.10) | copy-start | bytes 196612
  249.5 281.4 %all-to-all-start.2 = ((bf16[32,32,256]{2,1,0:T(8,128)(2,1)}), bf16[32,32,256]{2,1,0:T(8,128)(2,1)}, u32[]{:S(2)}, u32[]{:S(2)}) async-start(bf16[32,32,256]{2,1,0:T(8,128)(2,1)} %bitcast.33), calls=%async_computation.2 | async-start | bytes 1048576 | tf_op jit(solution)/shard_map/all_to_all | solution.py:63
  258.9 270.4 %all-reduce.2.cloned.1.call-start = ((), (), s32[]{:S(2)}) async-start(), calls=%async_computation.3 | async-start | bytes 262144 | tf_op jit(solution)/shard_map/psum | solution.py:75
Sparse Core Ops, SparseCore 0:
  265.3 263.9 all-reduce.1
